TPU v7x, 32 devices: a whole 2x2x4 slice. The times are simulated.
32 devices in a mesh: groups: 2 (over x), lat: 8 (over z, y), rep: 2 (over core).
Axes of the slice: x: 2, y: 2, z: 4, core: 2. Of those that a mesh axis runs over, the one named last changes fastest.
Arguments:
- acts: bfloat16 [128, 2304], P(('groups', 'lat', 'rep')), parts along dimension 0, may hold values from -6 to 6
- dest: int32 [128], P(('groups', 'lat', 'rep')), parts along dimension 0, may hold values from 0 to 7, as said below
- counts: int32 [32], P(('groups', 'lat', 'rep')), parts along dimension 0, may hold values from 2 to 4, as said below
- w_gate: bfloat16 [2304, 9216], P(None, 'lat'), may hold values from -0.125 to 0.125
- w_up: bfloat16 [2304, 9216], P(None, 'lat'), may hold values from -0.125 to 0.125
- w_down: bfloat16 [9216, 2304], P('lat'), may hold values from -0.0625 to 0.0625
- enc_weight: float32 [2, 2304, 16384], P('rep', None, 'lat'), may hold values from -0.125 to 0.125
- enc_bias: float32 [2, 16384], P('rep', 'lat'), may hold values from -1.5 to 1.5
- dec_weight: float32 [2, 16384, 2304], P('rep', 'lat'), may hold values from -0.09375 to 0.09375
- dec_bias: float32 [2, 2304], P('rep'), may hold values from -3 to 3
Outputs:
- grad_dec: float32 [4, 16384, 2304], P(('groups', 'rep'), 'lat'), parts along dimension 0
There are 2 independent parts, one for each index of `groups`. A program takes and returns all parts, laid end to end along the dimension named above; an argument that names none is the same for every part. Nothing has to cross between parts.
Inputs may be any that keep to these rules, and one draw needn't show every extreme that they name: `dest`: Micro-batch m belongs to autoencoder m // 4. Of the valid rows held by the two devices of one lat index (row blocks 2l and 2l + 1), at most 6 go to each autoencoder; in every draw some lat index sends exactly 6 to autoencoder 0 and another exactly 6 to autoencoder 1. Every micro-batch holds at least one valid row. Entries of rows that are not valid carry no meaning. The valid rows of a block are its first counts[k] rows.
All inputs are finite; a program needn't handle non-finite values.
Results may differ from a plain program's by a relative error of at most 0.0029.
Values may be sent and summed in bfloat16 or wider, within the bound.
No kernel may reach another device: no remote copies, remote signals or barrier semaphores. Data moves between devices by JAX's collectives and lax.ppermute only.
A program may use at most 128 MiB of HBM per device.

v0:
```python
import functools

import jax
import jax.numpy as jnp
from jax import lax
from jax.experimental import pallas as pl
from jax.experimental.pallas import tpu as pltpu
from jax.sharding import PartitionSpec as P

MB_REP = 4
CAP = 6
SUB = 8
LANE = 128
BF = jnp.bfloat16
F4 = jnp.float32
CODER_BYTES = 46 << 20
GRAD_BYTES = 26 << 20


def dot(a, b):
    return jnp.dot(a, b, preferred_element_type=F4)


def split(x):
    high = x.astype(BF)
    return high, (x - high.astype(F4)).astype(BF)


def chunk_rows(extent, want):
    return want if extent % want == 0 else extent


def mlp_kernel(step, down_step, piece, gate_hbm, up_hbm, down_hbm, out, gate_v, up_v, down_v, gate_acc, up_acc, sems):
    depth, hidden_n = gate_v.shape
    width = down_v.shape[1]
    n, row_dev = piece.shape[:2]
    rows = n * row_dev
    copies = []
    for k in range(depth // step):
        part = pl.ds(k * step, step)
        copies.append(
            (
                pltpu.make_async_copy(gate_hbm.at[part], gate_v.at[part], sems.at[2 * k]),
                pltpu.make_async_copy(up_hbm.at[part], up_v.at[part], sems.at[2 * k + 1]),
            )
        )
    base = 2 * (depth // step)
    downs = []
    for k in range(hidden_n // down_step):
        part = pl.ds(k * down_step, down_step)
        downs.append(pltpu.make_async_copy(down_hbm.at[part], down_v.at[part], sems.at[base + k]))
    for pair in copies:
        pair[0].start()
        pair[1].start()
    for copy in downs:
        copy.start()
    whole = jnp.concatenate([piece[s].astype(F4) for s in range(n)], axis=0).astype(BF)
    for k, pair in enumerate(copies):
        part = pl.ds(k * step, step)
        left = whole[:, k * step : (k + 1) * step]
        pair[0].wait()
        gate_part = dot(left, gate_v[part, :])
        pair[1].wait()
        up_part = dot(left, up_v[part, :])
        if k == 0:
            gate_acc[...] = gate_part
            up_acc[...] = up_part
        else:
            gate_acc[...] += gate_part
            up_acc[...] += up_part
    hidden = (jax.nn.gelu(gate_acc[...], approximate=True) * up_acc[...]).astype(BF)
    total = None
    for k, copy in enumerate(downs):
        copy.wait()
        part = dot(hidden[:, k * down_step : (k + 1) * down_step], down_v[pl.ds(k * down_step, down_step), :])
        total = part if total is None else total + part
    across = width // LANE
    share = out.shape[1]
    for t in range(rows // SUB * across):
        g, j = divmod(t, across)
        out[t // share, t % share] = total[g * SUB : (g + 1) * SUB, j * LANE : (j + 1) * LANE]


def coder_kernel(
    rows_side, step, down_step,
    own, other, biases, enc_hbm, dec_hbm,
    partial, codes_out,
    enc_v, dec_v, feats, acc, recon, sems,
):
    depth, latents = enc_v.shape
    width = dec_v.shape[1]
    across = width // LANE
    slots = acc.shape[0]
    encs, decs = [], []
    for k in range(depth // step):
        part = pl.ds(k * step, step)
        encs.append(pltpu.make_async_copy(enc_hbm.at[0, part], enc_v.at[part], sems.at[k]))
    for k in range(latents // down_step):
        part = pl.ds(k * down_step, down_step)
        decs.append(pltpu.make_async_copy(dec_hbm.at[0, part], dec_v.at[part], sems.at[len(encs) + k]))
    for copy in encs + decs:
        copy.start()

    share = own.shape[1] - 1
    labels = []
    for side, source in enumerate((own, other)):
        for g in range(rows_side // SUB):
            labels.append(source[2 * g, share].astype(F4) + source[2 * g + 1, share].astype(F4))
            for j in range(across):
                t = g * across + j
                feats[side * rows_side + g * SUB : side * rows_side + (g + 1) * SUB, j * LANE : (j + 1) * LANE] = source[t // share, t % share].astype(F4)
    label = jnp.concatenate(labels, axis=0)
    every = label.shape[0]
    first = (lax.axis_index("rep") * MB_REP).astype(F4) + 1.0
    keep = jnp.where((label >= first) & (label < first + MB_REP), 1.0, 0.0)
    row_of = lax.broadcasted_iota(jnp.int32, (every, every), 0)
    column_of = lax.broadcasted_iota(jnp.int32, (every, every), 1)
    keep_wide = jnp.broadcast_to(keep[:, :1], (every, every))
    keep_row = jnp.sum(jnp.where(row_of == column_of, keep_wide, 0.0), axis=0, keepdims=True)
    before = jnp.sum(jnp.where(row_of < column_of, keep_wide, 0.0), axis=0, keepdims=True)
    slot_of = lax.broadcasted_iota(jnp.int32, (slots, every), 0).astype(F4)
    picked = jnp.where((before == slot_of) & (keep_row > 0.0), 1.0, 0.0).astype(BF)
    slot_label = dot(picked, label.astype(BF))
    weight = jnp.zeros_like(slot_label)
    for m in range(MB_REP):
        size = jnp.sum(jnp.where(label == first + m, 1.0, 0.0), axis=0, keepdims=True)
        weight = weight + jnp.where(slot_label == first + m, 1.0 / jnp.maximum(size, 1.0), 0.0)
    twice = 2.0 * weight[:, :1]
    batch = dot(picked, feats[...].astype(BF))
    feats[0:slots, :] = batch

    for k, copy in enumerate(encs):
        left = batch[:, k * step : (k + 1) * step].astype(BF)
        copy.wait()
        high, low = split(enc_v[pl.ds(k * step, step), :])
        part = dot(left, high) + dot(left, low)
        if k == 0:
            acc[...] = part + biases[:, :latents]
        else:
            acc[...] += part
    codes = jnp.maximum(acc[...], 0.0)
    code_high, code_low = split(codes)
    out_high, out_low = split(twice * codes)
    codes_out[0:slots, :] = out_high
    codes_out[slots : 2 * slots, :] = out_low
    stacked = jnp.concatenate([code_high, code_low], axis=0)
    for k, copy in enumerate(decs):
        part = slice(k * down_step, (k + 1) * down_step)
        copy.wait()
        high, low = split(dec_v[pl.ds(k * down_step, down_step), :])
        both = dot(stacked[:, part], high)
        here = both[:slots] + both[slots:] + dot(code_high[:, part], low)
        if k == 0:
            recon[...] = here
        else:
            recon[...] += here
    leads = lax.axis_index("lat") == 0
    local = recon[...] + jnp.where(leads, biases[:, latents:] - feats[0:slots, :], 0.0)
    out_share = partial.shape[1]
    tiles = slots // SUB * across
    for t in range(partial.shape[0] * out_share):
        if t < tiles:
            g, j = divmod(t, across)
            partial[t // out_share, t % out_share] = local[g * SUB : (g + 1) * SUB, j * LANE : (j + 1) * LANE]
        else:
            partial[t // out_share, t % out_share] = jnp.zeros((SUB, LANE), F4)


def grad_kernel(block, err, codes, out, stacked, held, sems):
    slots = stacked.shape[0] // 2
    latents, width = held.shape
    across = width // LANE
    share = err.shape[1]
    for t in range(slots // SUB * across):
        g, j = divmod(t, across)
        tile = err[t // share, t % share]
        for half in (0, slots):
            stacked[half + g * SUB : half + (g + 1) * SUB, j * LANE : (j + 1) * LANE] = tile
    copies = []
    for k in range(latents // block):
        part = pl.ds(k * block, block)
        held[part, :] = lax.dot_general(
            codes[:, k * block : (k + 1) * block], stacked[...], (((0,), (0,)), ((), ())), preferred_element_type=F4
        )
        copies.append(pltpu.make_async_copy(held.at[part], out.at[0, part], sems.at[k]))
        copies[-1].start()
    for copy in copies:
        copy.wait()


def exchange(blocks):
    return lax.all_to_all(blocks, "lat", 0, 0)


def to_all(block, n):
    return exchange(jnp.broadcast_to(block[None], (n, *block.shape)))


def shards(acts, dest, counts, w_gate, w_up, w_down, enc_weight, enc_bias, dec_weight, dec_bias):
    n = lax.axis_size("lat")
    row_dev, depth = acts.shape
    hidden_n = w_gate.shape[1]
    width = w_down.shape[1]
    latents = enc_weight.shape[2]
    across = width // LANE
    rows = n * row_dev
    share = rows // SUB * across // n
    slots = n * CAP
    out_share = pl.cdiv(slots // SUB * across, n)
    anywhere = pl.BlockSpec(memory_space=pl.ANY)
    in_vmem = pl.BlockSpec(memory_space=pltpu.VMEM)

    piece = to_all(acts, n)
    step, down_step = chunk_rows(depth, 768), chunk_rows(hidden_n, 128)
    summed = pl.pallas_call(
        functools.partial(mlp_kernel, step, down_step),
        out_shape=jax.ShapeDtypeStruct((n, share, SUB, LANE), F4),
        in_specs=[in_vmem, anywhere, anywhere, anywhere],
        out_specs=in_vmem,
        scratch_shapes=[
            pltpu.VMEM((depth, hidden_n), BF),
            pltpu.VMEM((depth, hidden_n), BF),
            pltpu.VMEM((hidden_n, width), BF),
            pltpu.VMEM((rows, hidden_n), F4),
            pltpu.VMEM((rows, hidden_n), F4),
            pltpu.SemaphoreType.DMA((2 * (depth // step) + hidden_n // down_step,)),
        ],
        name="mlp",
    )(piece, w_gate, w_up, w_down)
    feats = jnp.sum(exchange(summed), axis=0).astype(BF)

    spot = jnp.arange(SUB, dtype=jnp.int32) - (lax.axis_index("lat") * row_dev) % SUB
    here = jnp.arange(row_dev, dtype=jnp.int32)
    tags = jnp.where(here < counts[0], dest + 1, 0)
    mark = jnp.sum(jnp.where(spot[:, None] == here[None, :], tags[None, :], 0), axis=1)
    mark = jnp.broadcast_to(mark[:, None], (SUB, LANE)).astype(BF)
    own = to_all(jnp.concatenate([feats, mark[None]], axis=0), n)
    other = lax.ppermute(own, "rep", [(0, 1), (1, 0)])

    step, down_step = chunk_rows(depth, 256), chunk_rows(latents, 256)
    partial, codes = pl.pallas_call(
        functools.partial(coder_kernel, rows, step, down_step),
        out_shape=(
            jax.ShapeDtypeStruct((n, out_share, SUB, LANE), F4),
            jax.ShapeDtypeStruct((2 * slots, latents), BF),
        ),
        in_specs=[in_vmem, in_vmem, in_vmem, anywhere, anywhere],
        out_specs=(in_vmem, in_vmem),
        scratch_shapes=[
            pltpu.VMEM((depth, latents), F4),
            pltpu.VMEM((latents, width), F4),
            pltpu.VMEM((2 * rows, width), F4),
            pltpu.VMEM((slots, latents), F4),
            pltpu.VMEM((slots, width), F4),
            pltpu.SemaphoreType.DMA((depth // step + latents // down_step,)),
        ],
        compiler_params=pltpu.CompilerParams(vmem_limit_bytes=CODER_BYTES),
        name="coder",
    )(own, other, jnp.concatenate([enc_bias, dec_bias], axis=1), enc_weight, dec_weight)
    err = to_all(jnp.sum(exchange(partial), axis=0).astype(BF), n)

    block = chunk_rows(latents, 128)
    return pl.pallas_call(
        functools.partial(grad_kernel, block),
        out_shape=jax.ShapeDtypeStruct((1, latents, width), F4),
        in_specs=[in_vmem, in_vmem],
        out_specs=anywhere,
        scratch_shapes=[
            pltpu.VMEM((2 * slots, width), BF),
            pltpu.VMEM((latents, width), F4),
            pltpu.SemaphoreType.DMA((latents // block,)),
        ],
        compiler_params=pltpu.CompilerParams(vmem_limit_bytes=GRAD_BYTES),
        name="grad",
    )(err, codes)


def solution(mesh):
    placed = (
        P(("groups", "lat", "rep"), None),
        P(("groups", "lat", "rep")),
        P(("groups", "lat", "rep")),
        P(None, "lat"),
        P(None, "lat"),
        P("lat", None),
        P("rep", None, "lat"),
        P("rep", "lat"),
        P("rep", "lat", None),
        P("rep", None),
    )
    return jax.shard_map(
        shards,
        mesh=mesh,
        in_specs=placed,
        out_specs=P(("groups", "rep"), "lat", None),
        check_vma=False,
    )
```

profile of v0, /device:TPU:0, one launch (start us, length us, event | category | flops | bytes accessed | tf_op | source)
XLA Modules:
  0.0 95.2 jit_solution(10776800008024196306)
XLA Ops:
  0.0 0.8 broadcast_in_dim.24
  0.8 14.7 %all_to_all.25.piece = bf16[8,4,2304]{2,1,0:T(4,128)(2,1)} all-to-all(bf16[8,4,2304]{2,1,0:T(4,128)(2,1)S(1)} %broadcast_in_dim.24), channel_id=1, replica_groups=mesh['groups'=2,'lat'=8,'rep'=2] {'lat'}, dimensions={0} | all-to-all | bytes 294912 | tf_op jit(solution)/shard_map/all_to_all | solution.py:192
  15.4 7.5 %mlp.1 = f32[8,9,8,128]{3,2,1,0:T(8,128)} custom-call(bf16[8,4,2304]{2,1,0:T(4,128)(2,1)} %all_to_all.25.piece, bf16[2304,1152]{1,0:T(8,128)(2,1)} %gate_hbm.1, bf16[2304,1152]{1,0:T(8,128)(2,1)} %up_hbm.1, bf16[1152,2304]{1,0:T(8,128)(2,1)} %down_hbm.1), custom_call_target="tpu_custom_call" | custom-call | tf_op jit(solution)/shard_map/mlp/pallas_call | solution.py:215
  23.0 3.4 %all-to-all-start.1 = ((f32[8,9,8,128]{3,2,1,0:T(8,128)}), f32[8,9,8,128]{3,2,1,0:T(8,128)S(1)}, u32[]{:S(2)}, u32[]{:S(2)}) async-start(f32[8,9,8,128]{3,2,1,0:T(8,128)} %mlp.1), calls=%async_computation.1 | async-start | bytes 589824 | tf_op jit(solution)/shard_map/all_to_all | solution.py:192
  27.1 0.7 compare_select_fusion
  27.7 0.1 select_reduce_fusion
  27.8 7.0 %all-to-all-done.1 = f32[8,9,8,128]{3,2,1,0:T(8,128)S(1)} async-done(((f32[8,9,8,128]{3,2,1,0:T(8,128)}), f32[8,9,8,128]{3,2,1,0:T(8,128)S(1)}, u32[]{:S(2)}, u32[]{:S(2)}) %all-to-all-start.1) | async-done | bytes 294944 | tf_op jit(solution)/shard_map/all_to_all | solution.py:192
  34.9 0.1 broadcast_in_dim.28
  35.0 10.9 %all_to_all.26.own = bf16[8,10,8,128]{3,2,1,0:T(8,128)(2,1)S(1)} all-to-all(bf16[8,10,8,128]{3,2,1,0:T(8,128)(2,1)S(1)} %broadcast_in_dim.29), channel_id=1, replica_groups=mesh['groups'=2,'lat'=8,'rep'=2] {'lat'}, dimensions={0} | all-to-all | bytes 327680 | tf_op jit(solution)/shard_map/all_to_all | solution.py:192
  45.9 0.0 collective-permute-start
  45.9 0.7 pad_maximum_fusion.1.biases
  46.6 0.7 collective-permute-done.other
  47.2 12.6 %coder.1 = (f32[8,14,8,128]{3,2,1,0:T(8,128)S(1)}, bf16[96,2048]{1,0:T(8,128)(2,1)S(1)}) custom-call(bf16[8,10,8,128]{3,2,1,0:T(8,128)(2,1)S(1)} %all_to_all.26.own, bf16[8,10,8,128]{3,2,1,0:T(8,128)(2,1)S(1)} %collective-permute-done.other, f32[1,4352]{1,0:T(1,128)S(1)} %pad_maximum_fusion.1.biases, f32[1,2304,2048]{2,1,0:T(8,128)} %enc_hbm.1, ...), custom_call_target="tpu_custom_call" | custom-call | tf_op jit(solution)/shard_map/coder/pallas_call | solution.py:241
  59.9 16.2 %all_to_all.27 = f32[8,14,8,128]{3,2,1,0:T(8,128)S(1)} all-to-all(f32[8,14,8,128]{3,2,1,0:T(8,128)S(1)} %get-tuple-element.7), channel_id=1, replica_groups=mesh['groups'=2,'lat'=8,'rep'=2] {'lat'}, dimensions={0} | all-to-all | bytes 917504 | tf_op jit(solution)/shard_map/all_to_all | solution.py:192
  76.1 11.9 %all_to_all.28.err = bf16[8,14,8,128]{3,2,1,0:T(8,128)(2,1)S(1)} all-to-all(bf16[8,14,8,128]{3,2,1,0:T(8,128)(2,1)S(1)} %broadcast_in_dim.50), channel_id=1, replica_groups=mesh['groups'=2,'lat'=8,'rep'=2] {'lat'}, dimensions={0} | all-to-all | bytes 458752 | tf_op jit(solution)/shard_map/all_to_all | solution.py:192
  88.0 7.0 %grad.1 = f32[1,2048,2304]{2,1,0:T(8,128)} custom-call(bf16[8,14,8,128]{3,2,1,0:T(8,128)(2,1)S(1)} %all_to_all.28.err, bf16[96,2048]{1,0:T(8,128)(2,1)S(1)} %get-tuple-element.8.codes), custom_call_target="tpu_custom_call" | custom-call | tf_op jit(solution)/shard_map/grad/pallas_call | solution.py:263
  (7 shorter events, 0.1 us)
Async XLA Ops:
  23.0 11.9 %all-to-all-start.1 = ((f32[8,9,8,128]{3,2,1,0:T(8,128)}), f32[8,9,8,128]{3,2,1,0:T(8,128)S(1)}, u32[]{:S(2)}, u32[]{:S(2)}) async-start(f32[8,9,8,128]{3,2,1,0:T(8,128)} %mlp.1), calls=%async_computation.1 | async-start | bytes 589824 | tf_op jit(solution)/shard_map/all_to_all | solution.py:192
  45.9 1.4 %collective-permute-start = (bf16[8,10,8,128]{3,2,1,0:T(8,128)(2,1)S(1)}, bf16[8,10,8,128]{3,2,1,0:T(8,128)(2,1)S(1)}, u32[]{:S(2)}, u32[]{:S(2)}) collective-permute-start(bf16[8,10,8,128]{3,2,1,0:T(8,128)(2,1)S(1)} %all_to_all.26.own), channel_id=1, source_target_pairs={{0,1},{1,0},{2,3},{3,2},{4,5},{5,4},{6,7},{7,6},{8,9},{9,8},{10,11... | collective-permute-start | bytes 491528 | tf_op jit(solution)/shard_map/ppermute | solution.py:238
where the time goes:
time: 95.7 us; the launch traced here: 95.2 us
  blocking collectives  53.6 us (56%)
  Pallas kernels  27.1 us (28%)
  waiting for transfers between devices  7.69 us (8%)
  starting transfers between devices  3.44 us (4%)
  other arithmetic  1.55 us (2%)
    all_to_all x4, blocking collectives, exchange(): return lax.all_to_all(blocks, 'lat', 0, 0)  53.6 us
    pallas_call x1, Pallas kernels, shards(): pl.pallas_call(functools.partial(coder_kernel, rows, step, down_step), ou...  12.6 us
    pallas_call x1, Pallas kernels, shards(): pl.pallas_call(functools.partial(mlp_kernel, step, down_step), out_shape=...  7.52 us
    all_to_all x1, waiting for transfers between devices, exchange(): return lax.all_to_all(blocks, 'lat', 0, 0)  7.03 us
    pallas_call x1, Pallas kernels, shards(): pl.pallas_call(functools.partial(grad_kernel, block), out_shape=jax.Shape...  6.97 us
    all_to_all x1, starting transfers between devices, exchange(): return lax.all_to_all(blocks, 'lat', 0, 0)  3.43 us
  transfers between devices with their start and end apart: 2, of which 2 were waited for; matrix products, arithmetic and copies ran while one was open for 2% of the time, Pallas kernels for 0%

commit v1 on v0

--- a/solution.py
+++ b/solution.py
@@ -11,10 +11,12 @@
 CAP = 6
 SUB = 8
 LANE = 128
+LIMIT = 32767.0
 BF = jnp.bfloat16
 F4 = jnp.float32
 CODER_BYTES = 46 << 20
 GRAD_BYTES = 26 << 20
+GLUE_BYTES = 2 << 20
 
 
 def dot(a, b):
@@ -30,11 +32,77 @@
     return want if extent % want == 0 else extent
 
 
+def encode(local, out):
+    share = out.shape[1] - 1
+    across = local.shape[1] // LANE
+    groups = local.shape[0] // SUB
+    peak = jnp.max(jnp.abs(local), axis=1, keepdims=True)
+    power = jnp.clip(jnp.ceil(jnp.log2(jnp.maximum(peak, 1e-30))), -96.0, 120.0)
+    codes = jnp.clip(jnp.round(local * jnp.exp2(15.0 - power)), -LIMIT, LIMIT).astype(jnp.int32)
+    lane = lax.broadcasted_iota(jnp.int32, (SUB, LANE), 1)
+    powers = jnp.zeros((SUB, LANE), F4)
+    for g in range(groups):
+        powers = jnp.where(lane == g, power[g * SUB : (g + 1) * SUB], powers)
+    powers = powers.astype(jnp.int32).astype(jnp.int16)
+    for t in range(out.shape[0] * share):
+        if t < groups * across:
+            g, j = divmod(t, across)
+            out[t // share, t % share] = codes[g * SUB : (g + 1) * SUB, j * LANE : (j + 1) * LANE].astype(jnp.int16)
+        else:
+            out[t // share, t % share] = jnp.zeros((SUB, LANE), jnp.int16)
+    for s in range(out.shape[0]):
+        out[s, share] = powers
+
+
+def decode(parts, across):
+    n, share = parts.shape[0], parts.shape[1] - 1
+    start = lax.axis_index("lat") * share
+    first = lax.div(start, across)
+    lane = lax.broadcasted_iota(jnp.int32, (SUB, LANE), 1)
+    units = []
+    for s in range(n):
+        scale = jnp.exp2(parts[s, share].astype(jnp.int32).astype(F4) - 15.0)
+        units.append(
+            [
+                jnp.broadcast_to(jnp.sum(jnp.where(lane == first + h, scale, 0.0), axis=1, keepdims=True), (SUB, LANE))
+                for h in range((share + across - 2) // across + 1)
+            ]
+        )
+    tiles = []
+    for t in range(share):
+        ahead = lax.div(start + t, across) - first
+        total = None
+        for s in range(n):
+            unit = units[s][0]
+            for h in range(1, len(units[s])):
+                unit = jnp.where(ahead == h, units[s][h], unit)
+            value = parts[s, t].astype(jnp.int32).astype(F4) * unit
+            total = value if total is None else total + value
+        tiles.append(total.astype(BF))
+    return tiles
+
+
+def feats_kernel(across, row_dev, parts, mark, out):
+    tiles = decode(parts, across)
+    turn = lax.broadcasted_iota(jnp.int32, (SUB, LANE), 0) // row_dev
+    mine = turn == lax.rem(lax.axis_index("lat"), SUB // row_dev)
+    tags = jnp.where(mine, mark[...], 0.0).astype(BF)
+    for s in range(parts.shape[0]):
+        for t, tile in enumerate(tiles):
+            out[s, t] = tile
+        out[s, len(tiles)] = tags
+
+
+def err_kernel(across, parts, out):
+    tiles = decode(parts, across)
+    for s in range(parts.shape[0]):
+        for t, tile in enumerate(tiles):
+            out[s, t] = tile
+
+
 def mlp_kernel(step, down_step, piece, gate_hbm, up_hbm, down_hbm, out, gate_v, up_v, down_v, gate_acc, up_acc, sems):
     depth, hidden_n = gate_v.shape
-    width = down_v.shape[1]
-    n, row_dev = piece.shape[:2]
-    rows = n * row_dev
+    n = piece.shape[0]
     copies = []
     for k in range(depth // step):
         part = pl.ds(k * step, step)
@@ -74,11 +142,7 @@
         copy.wait()
         part = dot(hidden[:, k * down_step : (k + 1) * down_step], down_v[pl.ds(k * down_step, down_step), :])
         total = part if total is None else total + part
-    across = width // LANE
-    share = out.shape[1]
-    for t in range(rows // SUB * across):
-        g, j = divmod(t, across)
-        out[t // share, t % share] = total[g * SUB : (g + 1) * SUB, j * LANE : (j + 1) * LANE]
+    encode(total, out)
 
 
 def coder_kernel(
@@ -156,14 +220,7 @@
             recon[...] += here
     leads = lax.axis_index("lat") == 0
     local = recon[...] + jnp.where(leads, biases[:, latents:] - feats[0:slots, :], 0.0)
-    out_share = partial.shape[1]
-    tiles = slots // SUB * across
-    for t in range(partial.shape[0] * out_share):
-        if t < tiles:
-            g, j = divmod(t, across)
-            partial[t // out_share, t % out_share] = local[g * SUB : (g + 1) * SUB, j * LANE : (j + 1) * LANE]
-        else:
-            partial[t // out_share, t % out_share] = jnp.zeros((SUB, LANE), F4)
+    encode(local, partial)
 
 
 def grad_kernel(block, err, codes, out, stacked, held, sems):
@@ -214,7 +271,7 @@
     step, down_step = chunk_rows(depth, 768), chunk_rows(hidden_n, 128)
     summed = pl.pallas_call(
         functools.partial(mlp_kernel, step, down_step),
-        out_shape=jax.ShapeDtypeStruct((n, share, SUB, LANE), F4),
+        out_shape=jax.ShapeDtypeStruct((n, share + 1, SUB, LANE), jnp.int16),
         in_specs=[in_vmem, anywhere, anywhere, anywhere],
         out_specs=in_vmem,
         scratch_shapes=[
@@ -227,21 +284,27 @@
         ],
         name="mlp",
     )(piece, w_gate, w_up, w_down)
-    feats = jnp.sum(exchange(summed), axis=0).astype(BF)
-
-    spot = jnp.arange(SUB, dtype=jnp.int32) - (lax.axis_index("lat") * row_dev) % SUB
-    here = jnp.arange(row_dev, dtype=jnp.int32)
-    tags = jnp.where(here < counts[0], dest + 1, 0)
-    mark = jnp.sum(jnp.where(spot[:, None] == here[None, :], tags[None, :], 0), axis=1)
-    mark = jnp.broadcast_to(mark[:, None], (SUB, LANE)).astype(BF)
-    own = to_all(jnp.concatenate([feats, mark[None]], axis=0), n)
+    parts = exchange(summed)
+
+    tags = jnp.where(jnp.arange(row_dev, dtype=jnp.int32) < counts[0], dest + 1, 0)
+    mark = jnp.broadcast_to(jnp.tile(tags, SUB // row_dev)[:, None], (SUB, LANE)).astype(F4)
+    own = exchange(
+        pl.pallas_call(
+            functools.partial(feats_kernel, across, row_dev),
+            out_shape=jax.ShapeDtypeStruct((n, share + 1, SUB, LANE), BF),
+            in_specs=[in_vmem, in_vmem],
+            out_specs=in_vmem,
+            compiler_params=pltpu.CompilerParams(vmem_limit_bytes=GLUE_BYTES),
+            name="feats",
+        )(parts, mark)
+    )
     other = lax.ppermute(own, "rep", [(0, 1), (1, 0)])
 
     step, down_step = chunk_rows(depth, 256), chunk_rows(latents, 256)
     partial, codes = pl.pallas_call(
         functools.partial(coder_kernel, rows, step, down_step),
         out_shape=(
-            jax.ShapeDtypeStruct((n, out_share, SUB, LANE), F4),
+            jax.ShapeDtypeStruct((n, out_share + 1, SUB, LANE), jnp.int16),
             jax.ShapeDtypeStruct((2 * slots, latents), BF),
         ),
         in_specs=[in_vmem, in_vmem, in_vmem, anywhere, anywhere],
@@ -257,7 +320,16 @@
         compiler_params=pltpu.CompilerParams(vmem_limit_bytes=CODER_BYTES),
         name="coder",
     )(own, other, jnp.concatenate([enc_bias, dec_bias], axis=1), enc_weight, dec_weight)
-    err = to_all(jnp.sum(exchange(partial), axis=0).astype(BF), n)
+    err = exchange(
+        pl.pallas_call(
+            functools.partial(err_kernel, across),
+            out_shape=jax.ShapeDtypeStruct((n, out_share, SUB, LANE), BF),
+            in_specs=[in_vmem],
+            out_specs=in_vmem,
+            compiler_params=pltpu.CompilerParams(vmem_limit_bytes=GLUE_BYTES),
+            name="err",
+        )(exchange(partial))
+    )
 
     block = chunk_rows(latents, 128)
     return pl.pallas_call(

time: 95.7 us -> 89.5 us (0.935)
  blocking collectives: 53.6 us -> 48.1 us
    all_to_all x4, blocking collectives: 53.6 us -> 48.1 us  [exchange(): return lax.all_to_all(blocks, 'lat', 0, 0)]
where the time goes in v1:
time: 89.5 us; the launch traced here: 89.1 us
  blocking collectives  48.1 us (54%)
  Pallas kernels  27.6 us (31%)
  waiting for transfers between devices  6.76 us (8%)
  starting transfers between devices  3.4 us (4%)
  other arithmetic  1.39 us (2%)
  local copies, waits for them, and re-layouts  0.92 us (1%)
    all_to_all x4, blocking collectives, exchange(): return lax.all_to_all(blocks, 'lat', 0, 0)  48.1 us
    pallas_call x1, Pallas kernels, shards(): pl.pallas_call(functools.partial(coder_kernel, rows, step, down_step), ou...  12.8 us
    pallas_call x1, Pallas kernels, shards(): pl.pallas_call(functools.partial(mlp_kernel, step, down_step), out_shape=...  7.6 us
    pallas_call x1, Pallas kernels, shards(): pl.pallas_call(functools.partial(grad_kernel, block), out_shape=jax.Shape...  6.97 us
    all_to_all x1, waiting for transfers between devices, exchange(): return lax.all_to_all(blocks, 'lat', 0, 0)  6.1 us
    all_to_all x1, starting transfers between devices, exchange(): return lax.all_to_all(blocks, 'lat', 0, 0)  3.39 us
  transfers between devices with their start and end apart: 2, of which 2 were waited for; matrix products, arithmetic and copies ran while one was open for 2% of the time, Pallas kernels for 0%

profile of v1, /device:TPU:0, one launch (start us, length us, event | category | flops | bytes accessed | tf_op | source)
XLA Modules:
  0.0 89.1 jit_solution(10272344348402122168)
XLA Ops:
  0.0 0.8 broadcast_in_dim.8
  0.8 14.7 %all_to_all.25.piece = bf16[8,4,2304]{2,1,0:T(4,128)(2,1)} all-to-all(bf16[8,4,2304]{2,1,0:T(4,128)(2,1)S(1)} %broadcast_in_dim.8), channel_id=1, replica_groups=mesh['groups'=2,'lat'=8,'rep'=2] {'lat'}, dimensions={0} | all-to-all | bytes 294912 | tf_op jit(solution)/shard_map/all_to_all | solution.py:249
  15.4 7.6 %mlp.1 = s16[8,10,8,128]{3,2,1,0:T(8,128)(2,1)} custom-call(bf16[8,4,2304]{2,1,0:T(4,128)(2,1)} %all_to_all.25.piece, bf16[2304,1152]{1,0:T(8,128)(2,1)} %gate_hbm.1, bf16[2304,1152]{1,0:T(8,128)(2,1)} %up_hbm.1, bf16[1152,2304]{1,0:T(8,128)(2,1)} %down_hbm.1), custom_call_target="tpu_custom_call" | custom-call | tf_op jit(solution)/shard_map/mlp/pallas_call | solution.py:272
  23.0 3.4 %all-to-all-start.1 = ((s16[8,10,8,128]{3,2,1,0:T(8,128)(2,1)}), s16[8,10,8,128]{3,2,1,0:T(8,128)(2,1)S(1)}, u32[]{:S(2)}, u32[]{:S(2)}) async-start(s16[8,10,8,128]{3,2,1,0:T(8,128)(2,1)} %mlp.1), calls=%async_computation.1 | async-start | bytes 327680 | tf_op jit(solution)/shard_map/all_to_all | solution.py:249
  27.1 0.7 fusion
  27.8 0.1 convert_element_type.6
  27.8 6.1 %all-to-all-done.1.parts = s16[8,10,8,128]{3,2,1,0:T(8,128)(2,1)S(1)} async-done(((s16[8,10,8,128]{3,2,1,0:T(8,128)(2,1)}), s16[8,10,8,128]{3,2,1,0:T(8,128)(2,1)S(1)}, u32[]{:S(2)}, u32[]{:S(2)}) %all-to-all-start.1) | async-done | bytes 163872 | tf_op jit(solution)/shard_map/all_to_all | solution.py:249
  33.9 0.1 broadcast_in_dim.17.mark
  34.0 0.1 feats.1
  34.1 10.0 %all_to_all.26.own = bf16[8,10,8,128]{3,2,1,0:T(8,128)(2,1)S(1)} all-to-all(bf16[8,10,8,128]{3,2,1,0:T(8,128)(2,1)S(1)} %feats.1), channel_id=1, replica_groups=mesh['groups'=2,'lat'=8,'rep'=2] {'lat'}, dimensions={0} | all-to-all | bytes 327680 | tf_op jit(solution)/shard_map/all_to_all | solution.py:249
  44.1 0.0 collective-permute-start
  44.1 0.7 pad_maximum_fusion.biases
  44.8 0.7 collective-permute-done.other
  45.5 12.8 %coder.1 = (s16[8,15,8,128]{3,2,1,0:T(8,128)(2,1)S(1)}, bf16[96,2048]{1,0:T(8,128)(2,1)S(1)}) custom-call(bf16[8,10,8,128]{3,2,1,0:T(8,128)(2,1)S(1)} %all_to_all.26.own, bf16[8,10,8,128]{3,2,1,0:T(8,128)(2,1)S(1)} %collective-permute-done.other, f32[1,4352]{1,0:T(1,128)S(1)} %pad_maximum_fusion.biases, f32[1,2304,2048]{2,1,0:T(8,128)} %enc_hbm.1, ...), custom_call_target="tpu_custom_call" | custom-call | tf_op jit(solution)/shard_map/coder/pallas_call | solution.py:304
  58.3 11.7 %all_to_all.27.parts = s16[8,15,8,128]{3,2,1,0:T(8,128)(2,1)S(1)} all-to-all(s16[8,15,8,128]{3,2,1,0:T(8,128)(2,1)S(1)} %get-tuple-element.7), channel_id=1, replica_groups=mesh['groups'=2,'lat'=8,'rep'=2] {'lat'}, dimensions={0} | all-to-all | bytes 491520 | tf_op jit(solution)/shard_map/all_to_all | solution.py:249
  70.0 0.2 err.1
  70.1 11.8 %all_to_all.28.err = bf16[8,14,8,128]{3,2,1,0:T(8,128)(2,1)S(1)} all-to-all(bf16[8,14,8,128]{3,2,1,0:T(8,128)(2,1)S(1)} %err.1), channel_id=1, replica_groups=mesh['groups'=2,'lat'=8,'rep'=2] {'lat'}, dimensions={0} | all-to-all | bytes 458752 | tf_op jit(solution)/shard_map/all_to_all | solution.py:249
  81.9 7.0 %grad.1 = f32[1,2048,2304]{2,1,0:T(8,128)} custom-call(bf16[8,14,8,128]{3,2,1,0:T(8,128)(2,1)S(1)} %all_to_all.28.err, bf16[96,2048]{1,0:T(8,128)(2,1)S(1)} %get-tuple-element.8.codes), custom_call_target="tpu_custom_call" | custom-call | tf_op jit(solution)/shard_map/grad/pallas_call | solution.py:335
  (1 shorter events, 0.0 us)
Async XLA Ops:
  23.0 10.9 %all-to-all-start.1 = ((s16[8,10,8,128]{3,2,1,0:T(8,128)(2,1)}), s16[8,10,8,128]{3,2,1,0:T(8,128)(2,1)S(1)}, u32[]{:S(2)}, u32[]{:S(2)}) async-start(s16[8,10,8,128]{3,2,1,0:T(8,128)(2,1)} %mlp.1), calls=%async_computation.1 | async-start | bytes 327680 | tf_op jit(solution)/shard_map/all_to_all | solution.py:249
  44.1 1.4 %collective-permute-start = (bf16[8,10,8,128]{3,2,1,0:T(8,128)(2,1)S(1)}, bf16[8,10,8,128]{3,2,1,0:T(8,128)(2,1)S(1)}, u32[]{:S(2)}, u32[]{:S(2)}) collective-permute-start(bf16[8,10,8,128]{3,2,1,0:T(8,128)(2,1)S(1)} %all_to_all.26.own), channel_id=1, source_target_pairs={{0,1},{1,0},{2,3},{3,2},{4,5},{5,4},{6,7},{7,6},{8,9},{9,8},{10,11... | collective-permute-start | bytes 491528 | tf_op jit(solution)/shard_map/ppermute | solution.py:301

commit v2 on v1

--- a/solution.py
+++ b/solution.py
@@ -17,6 +17,7 @@
 CODER_BYTES = 46 << 20
 GRAD_BYTES = 26 << 20
 GLUE_BYTES = 2 << 20
+MLP_BYTES = 8 << 20
 
 
 def dot(a, b):
@@ -82,6 +83,12 @@
     return tiles
 
 
+def spread_kernel(acts, *rest):
+    out = rest[-1]
+    for s in range(out.shape[0]):
+        out[s] = acts[...]
+
+
 def feats_kernel(across, row_dev, parts, mark, out):
     tiles = decode(parts, across)
     turn = lax.broadcasted_iota(jnp.int32, (SUB, LANE), 0) // row_dev
@@ -100,49 +107,12 @@
             out[s, t] = tile
 
 
-def mlp_kernel(step, down_step, piece, gate_hbm, up_hbm, down_hbm, out, gate_v, up_v, down_v, gate_acc, up_acc, sems):
-    depth, hidden_n = gate_v.shape
-    n = piece.shape[0]
-    copies = []
-    for k in range(depth // step):
-        part = pl.ds(k * step, step)
-        copies.append(
-            (
-                pltpu.make_async_copy(gate_hbm.at[part], gate_v.at[part], sems.at[2 * k]),
-                pltpu.make_async_copy(up_hbm.at[part], up_v.at[part], sems.at[2 * k + 1]),
-            )
-        )
-    base = 2 * (depth // step)
-    downs = []
-    for k in range(hidden_n // down_step):
-        part = pl.ds(k * down_step, down_step)
-        downs.append(pltpu.make_async_copy(down_hbm.at[part], down_v.at[part], sems.at[base + k]))
-    for pair in copies:
-        pair[0].start()
-        pair[1].start()
-    for copy in downs:
-        copy.start()
-    whole = jnp.concatenate([piece[s].astype(F4) for s in range(n)], axis=0).astype(BF)
-    for k, pair in enumerate(copies):
-        part = pl.ds(k * step, step)
-        left = whole[:, k * step : (k + 1) * step]
-        pair[0].wait()
-        gate_part = dot(left, gate_v[part, :])
-        pair[1].wait()
-        up_part = dot(left, up_v[part, :])
-        if k == 0:
-            gate_acc[...] = gate_part
-            up_acc[...] = up_part
-        else:
-            gate_acc[...] += gate_part
-            up_acc[...] += up_part
-    hidden = (jax.nn.gelu(gate_acc[...], approximate=True) * up_acc[...]).astype(BF)
-    total = None
-    for k, copy in enumerate(downs):
-        copy.wait()
-        part = dot(hidden[:, k * down_step : (k + 1) * down_step], down_v[pl.ds(k * down_step, down_step), :])
-        total = part if total is None else total + part
-    encode(total, out)
+def mlp_kernel(piece, gate_w, up_w, down_w, out):
+    left = jnp.concatenate([piece[s].astype(F4) for s in range(piece.shape[0])], axis=0).astype(BF)
+    gate = dot(left, gate_w[...])
+    up = dot(left, up_w[...])
+    hidden = (jax.nn.gelu(gate, approximate=True) * up).astype(BF)
+    encode(dot(hidden, down_w[...]), out)
 
 
 def coder_kernel(
@@ -249,10 +219,6 @@
     return lax.all_to_all(blocks, "lat", 0, 0)
 
 
-def to_all(block, n):
-    return exchange(jnp.broadcast_to(block[None], (n, *block.shape)))
-
-
 def shards(acts, dest, counts, w_gate, w_up, w_down, enc_weight, enc_bias, dec_weight, dec_bias):
     n = lax.axis_size("lat")
     row_dev, depth = acts.shape
@@ -267,21 +233,23 @@
     anywhere = pl.BlockSpec(memory_space=pl.ANY)
     in_vmem = pl.BlockSpec(memory_space=pltpu.VMEM)
 
-    piece = to_all(acts, n)
-    step, down_step = chunk_rows(depth, 768), chunk_rows(hidden_n, 128)
+    ahead = [pltpu.with_memory_space_constraint(w, pltpu.HBM) for w in (enc_weight, dec_weight)]
+    piece = exchange(
+        pl.pallas_call(
+            spread_kernel,
+            out_shape=jax.ShapeDtypeStruct((n, row_dev, depth), BF),
+            in_specs=[in_vmem] + [pl.BlockSpec(memory_space=pltpu.HBM)] * len(ahead),
+            out_specs=in_vmem,
+            compiler_params=pltpu.CompilerParams(vmem_limit_bytes=GLUE_BYTES),
+            name="spread",
+        )(acts, *ahead)
+    )
     summed = pl.pallas_call(
-        functools.partial(mlp_kernel, step, down_step),
+        mlp_kernel,
         out_shape=jax.ShapeDtypeStruct((n, share + 1, SUB, LANE), jnp.int16),
-        in_specs=[in_vmem, anywhere, anywhere, anywhere],
+        in_specs=[in_vmem] * 4,
         out_specs=in_vmem,
-        scratch_shapes=[
-            pltpu.VMEM((depth, hidden_n), BF),
-            pltpu.VMEM((depth, hidden_n), BF),
-            pltpu.VMEM((hidden_n, width), BF),
-            pltpu.VMEM((rows, hidden_n), F4),
-            pltpu.VMEM((rows, hidden_n), F4),
-            pltpu.SemaphoreType.DMA((2 * (depth // step) + hidden_n // down_step,)),
-        ],
+        compiler_params=pltpu.CompilerParams(vmem_limit_bytes=MLP_BYTES),
         name="mlp",
     )(piece, w_gate, w_up, w_down)
     parts = exchange(summed)

time: 89.5 us -> 85.4 us (0.954)
  Pallas kernels: 27.6 us -> 23.4 us
  other arithmetic: 1.39 us -> 0.02 us
  waiting for transfers between devices: 6.76 us -> 8.1 us
    pallas_call x1 -> x2, Pallas kernels: 7.6 us -> 3.37 us  [the longest x1 3.36 us: shards(): pl.pallas_call(mlp_kernel, out_shape=jax.ShapeDtypeStruct((n, share + 1,...]
  transfers between devices with their start and end apart: 2 -> 2, of which waited for: 2 -> 2; matrix products, arithmetic and copies ran while one was open for 2% -> 0% of each run, Pallas kernels for 0% -> 0%
where the time goes in v2:
time: 85.4 us; the launch traced here: 85.1 us
  blocking collectives  48.3 us (57%)
  Pallas kernels  23.4 us (27%)
  waiting for transfers between devices  8.1 us (9%)
  starting transfers between devices  3.38 us (4%)
  local copies, waits for them, and re-layouts  1.05 us (1%)
  between operations  0.88 us (1%)
    all_to_all x4, blocking collectives, exchange(): return lax.all_to_all(blocks, 'lat', 0, 0)  48.3 us
    pallas_call x1, Pallas kernels, shards(): pl.pallas_call(functools.partial(coder_kernel, rows, step, down_step), ou...  12.8 us
    pallas_call x1, Pallas kernels, shards(): pl.pallas_call(functools.partial(grad_kernel, block), out_shape=jax.Shape...  6.97 us
    all_to_all x1, waiting for transfers between devices, exchange(): return lax.all_to_all(blocks, 'lat', 0, 0)  6.74 us
    all_to_all x1, starting transfers between devices, exchange(): return lax.all_to_all(blocks, 'lat', 0, 0)  3.38 us
    pallas_call x1, Pallas kernels, shards(): pl.pallas_call(mlp_kernel, out_shape=jax.ShapeDtypeStruct((n, share + 1,...  3.36 us
  transfers between devices with their start and end apart: 2, of which 2 were waited for; matrix products, arithmetic and copies ran while one was open for 0% of the time, Pallas kernels for 0%

profile of v2, /device:TPU:0, one launch (start us, length us, event | category | flops | bytes accessed | tf_op | source)
XLA Modules:
  0.0 85.1 jit_solution(6519078318720404602)
XLA Ops:
  0.0 0.0 copy-start.2
  0.0 0.0 copy-start.1
  0.0 0.0 copy-start
  0.0 0.0 copy-start.3
  0.0 0.9 %copy-done.3 = bf16[4,2304]{1,0:T(4,128)(2,1)S(1)} copy-done((bf16[4,2304]{1,0:T(4,128)(2,1)S(1)}, bf16[4,2304]{1,0:T(4,128)(2,1)}, u32[]{:S(2)}) %copy-start.3) | copy-done | bytes 18456
  0.9 0.0 copy-start.6
  0.9 0.0 copy-start.4
  0.9 0.0 copy-start.5
  0.9 14.8 %all_to_all.25.piece = bf16[8,4,2304]{2,1,0:T(4,128)(2,1)S(1)} all-to-all(bf16[8,4,2304]{2,1,0:T(4,128)(2,1)S(1)} %spread.1), channel_id=1, replica_groups=mesh['groups'=2,'lat'=8,'rep'=2] {'lat'}, dimensions={0} | all-to-all | bytes 294912 | tf_op jit(solution)/shard_map/all_to_all | solution.py:219
  15.7 0.0 copy-done.2
  15.7 0.0 copy-done.1
  15.7 0.0 copy-done
  15.7 3.4 %mlp.1 = s16[8,10,8,128]{3,2,1,0:T(8,128)(2,1)} custom-call(bf16[8,4,2304]{2,1,0:T(4,128)(2,1)S(1)} %all_to_all.25.piece, bf16[2304,1152]{1,0:T(8,128)(2,1)S(1)} %copy-done, bf16[2304,1152]{1,0:T(8,128)(2,1)S(1)} %copy-done.1, bf16[1152,2304]{1,0:T(8,128)(2,1)S(1)} %copy-done.2), custom_call_target="tpu_custom_call" | custom-call | tf_op jit(solution)/shard_map/mlp/pallas_call | solution.py:247
  19.1 3.4 %all-to-all-start.1 = ((s16[8,10,8,128]{3,2,1,0:T(8,128)(2,1)}), s16[8,10,8,128]{3,2,1,0:T(8,128)(2,1)S(1)}, u32[]{:S(2)}, u32[]{:S(2)}) async-start(s16[8,10,8,128]{3,2,1,0:T(8,128)(2,1)} %mlp.1), calls=%async_computation.1 | async-start | bytes 327680 | tf_op jit(solution)/shard_map/all_to_all | solution.py:219
  23.1 0.0 copy-done.6
  23.2 0.1 convert_element_type.6
  23.2 6.7 %all-to-all-done.1.parts = s16[8,10,8,128]{3,2,1,0:T(8,128)(2,1)S(1)} async-done(((s16[8,10,8,128]{3,2,1,0:T(8,128)(2,1)}), s16[8,10,8,128]{3,2,1,0:T(8,128)(2,1)S(1)}, u32[]{:S(2)}, u32[]{:S(2)}) %all-to-all-start.1) | async-done | bytes 163872 | tf_op jit(solution)/shard_map/all_to_all | solution.py:219
  30.0 0.1 broadcast_in_dim.10.mark
  30.1 0.1 feats.1
  30.2 10.0 %all_to_all.26.own = bf16[8,10,8,128]{3,2,1,0:T(8,128)(2,1)S(1)} all-to-all(bf16[8,10,8,128]{3,2,1,0:T(8,128)(2,1)S(1)} %feats.1), channel_id=1, replica_groups=mesh['groups'=2,'lat'=8,'rep'=2] {'lat'}, dimensions={0} | all-to-all | bytes 327680 | tf_op jit(solution)/shard_map/all_to_all | solution.py:219
  40.2 0.0 collective-permute-start
  40.2 0.0 copy-done.4
  40.2 0.0 copy-done.5
  40.2 1.4 %collective-permute-done.other = bf16[8,10,8,128]{3,2,1,0:T(8,128)(2,1)S(1)} collective-permute-done((bf16[8,10,8,128]{3,2,1,0:T(8,128)(2,1)S(1)}, bf16[8,10,8,128]{3,2,1,0:T(8,128)(2,1)S(1)}, u32[]{:S(2)}, u32[]{:S(2)}) %collective-permute-start) | collective-permute-done | bytes 163872 | tf_op jit(solution)/shard_map/ppermute | solution.py:269
  41.5 12.8 %coder.1 = (s16[8,15,8,128]{3,2,1,0:T(8,128)(2,1)S(1)}, bf16[96,2048]{1,0:T(8,128)(2,1)S(1)}) custom-call(bf16[8,10,8,128]{3,2,1,0:T(8,128)(2,1)S(1)} %all_to_all.26.own, bf16[8,10,8,128]{3,2,1,0:T(8,128)(2,1)S(1)} %collective-permute-done.other, f32[1,4352]{1,0:T(1,128)S(1)} %pad_maximum_fusion.biases, f32[1,2304,2048]{2,1,0:T(8,128)} %enc_hbm.1, ...), custom_call_target="tpu_custom_call" | custom-call | tf_op jit(solution)/shard_map/coder/pallas_call | solution.py:272
  54.3 11.7 %all_to_all.27.parts = s16[8,15,8,128]{3,2,1,0:T(8,128)(2,1)S(1)} all-to-all(s16[8,15,8,128]{3,2,1,0:T(8,128)(2,1)S(1)} %get-tuple-element.7), channel_id=1, replica_groups=mesh['groups'=2,'lat'=8,'rep'=2] {'lat'}, dimensions={0} | all-to-all | bytes 491520 | tf_op jit(solution)/shard_map/all_to_all | solution.py:219
  66.0 0.2 err.1
  66.2 11.8 %all_to_all.28.err = bf16[8,14,8,128]{3,2,1,0:T(8,128)(2,1)S(1)} all-to-all(bf16[8,14,8,128]{3,2,1,0:T(8,128)(2,1)S(1)} %err.1), channel_id=1, replica_groups=mesh['groups'=2,'lat'=8,'rep'=2] {'lat'}, dimensions={0} | all-to-all | bytes 458752 | tf_op jit(solution)/shard_map/all_to_all | solution.py:219
  78.0 7.0 %grad.1 = f32[1,2048,2304]{2,1,0:T(8,128)} custom-call(bf16[8,14,8,128]{3,2,1,0:T(8,128)(2,1)S(1)} %all_to_all.28.err, bf16[96,2048]{1,0:T(8,128)(2,1)S(1)} %get-tuple-element.8.codes), custom_call_target="tpu_custom_call" | custom-call | tf_op jit(solution)/shard_map/grad/pallas_call | solution.py:303
  (4 shorter events, 0.0 us)
Async XLA Ops:
  0.0 15.7 %copy-start.2 = (bf16[1152,2304]{1,0:T(8,128)(2,1)S(1)}, bf16[1152,2304]{1,0:T(8,128)(2,1)}, u32[]{:S(2)}) copy-start(bf16[1152,2304]{1,0:T(8,128)(2,1)} %down_w.1) | copy-start | bytes 15925252
  0.0 15.7 %copy-start.1 = (bf16[2304,1152]{1,0:T(8,128)(2,1)S(1)}, bf16[2304,1152]{1,0:T(8,128)(2,1)}, u32[]{:S(2)}) copy-start(bf16[2304,1152]{1,0:T(8,128)(2,1)} %up_w.1) | copy-start | bytes 15925252
  0.0 15.7 %copy-start = (bf16[2304,1152]{1,0:T(8,128)(2,1)S(1)}, bf16[2304,1152]{1,0:T(8,128)(2,1)}, u32[]{:S(2)}) copy-start(bf16[2304,1152]{1,0:T(8,128)(2,1)} %gate_w.1) | copy-start | bytes 15925252
  0.0 0.9 %copy-start.3 = (bf16[4,2304]{1,0:T(4,128)(2,1)S(1)}, bf16[4,2304]{1,0:T(4,128)(2,1)}, u32[]{:S(2)}) copy-start(bf16[4,2304]{1,0:T(4,128)(2,1)} %acts.1) | copy-start | bytes 55300
  0.9 22.3 %copy-start.6 = (s32[4]{0:T(128)S(1)}, s32[4]{0:T(128)}, u32[]{:S(2)}) copy-start(s32[4]{0:T(128)} %param.11) | copy-start | bytes 52
  0.9 39.3 %copy-start.4 = (f32[1,2304]{1,0:T(1,128)S(1)}, f32[1,2304]{1,0:T(1,128)}, u32[]{:S(2)}) copy-start(f32[1,2304]{1,0:T(1,128)} %param.19) | copy-start | bytes 27652
  0.9 39.3 %copy-start.5 = (f32[1,2048]{1,0:T(1,128)S(1)}, f32[1,2048]{1,0:T(1,128)}, u32[]{:S(2)}) copy-start(f32[1,2048]{1,0:T(1,128)} %param.17) | copy-start | bytes 24580
  19.1 10.9 %all-to-all-start.1 = ((s16[8,10,8,128]{3,2,1,0:T(8,128)(2,1)}), s16[8,10,8,128]{3,2,1,0:T(8,128)(2,1)S(1)}, u32[]{:S(2)}, u32[]{:S(2)}) async-start(s16[8,10,8,128]{3,2,1,0:T(8,128)(2,1)} %mlp.1), calls=%async_computation.1 | async-start | bytes 327680 | tf_op jit(solution)/shard_map/all_to_all | solution.py:219
  40.2 1.4 %collective-permute-start = (bf16[8,10,8,128]{3,2,1,0:T(8,128)(2,1)S(1)}, bf16[8,10,8,128]{3,2,1,0:T(8,128)(2,1)S(1)}, u32[]{:S(2)}, u32[]{:S(2)}) collective-permute-start(bf16[8,10,8,128]{3,2,1,0:T(8,128)(2,1)S(1)} %all_to_all.26.own), channel_id=1, source_target_pairs={{0,1},{1,0},{2,3},{3,2},{4,5},{5,4},{6,7},{7,6},{8,9},{9,8},{10,11... | collective-permute-start | bytes 491528 | tf_op jit(solution)/shard_map/ppermute | solution.py:269
